TPU v7x, 32 devices: a whole 2x2x4 slice. The times are simulated.
32 devices in a mesh: leaf: 8 (over y, x, core), front: 4 (over z).
Axes of the slice: x: 2, y: 2, z: 4, core: 2. Of those that a mesh axis runs over, the one named last changes fastest.
Arguments:
- leaf_rhs: float32 [8, 64, 256], P('leaf', None, 'front'), may hold values from -6 to 6
- sep_rhs: float32 [8, 64, 256], P('leaf', None, 'front'), may hold values from -6 to 6
- leaf_inverse: float32 [8, 256, 256], P('leaf', 'front'), as said below
- sep_inverse: float32 [8, 256, 256], P('leaf', 'front')
- leaf_block: float32 [8, 32, 256], P('leaf', None, 'front'), may hold values from -0.375 to 0.375
- sep_block: float32 [8, 32, 256], P('leaf', None, 'front'), may hold values from -0.375 to 0.375
- pattern: int32 [2, 8, 32], replicated, may hold values from 0 to 255, as said below
- outer_solution: float32 [64, 256], P(None, 'front'), may hold values from -6 to 6
Outputs:
- solution: float32 [2, 8, 64, 256], P(None, 'leaf', None, 'front')
Inputs may be any that keep to these rules, and one draw needn't show every extreme that they name: `pattern`: within one supernode the 32 entries are distinct and rising, the first is 0 and the last is 255. `leaf_inverse`: each leaf block is lower triangular with its diagonal bounded away from zero.
All inputs are finite; a program needn't handle non-finite values.
Results may differ from a plain program's by a relative error of at most 0.0003.
Values sent between devices are 32-bit elements; how exact they have to be, the bound alone decides.
No kernel may reach another device: no remote copies, remote signals or barrier semaphores. Data moves between devices by JAX's collectives and lax.ppermute only.
A program may use at most 64 MiB of HBM per device.

v0:
```python
import jax
import jax.numpy as jnp
from jax import lax
from jax.sharding import PartitionSpec as P


def partner(block, axis, distance):
    count = lax.axis_size(axis)
    route = []
    for low in range(count):
        high = low | 1 << distance
        if high != low and high < count:
            route += [(low, high), (high, low)]
    return lax.ppermute(block, axis, route)


def times_rows(vectors, matrix):
    return jnp.dot(
        vectors, matrix, precision=lax.Precision.HIGHEST, preferred_element_type=jnp.float32
    )


def against_rows(vectors, matrix):
    return lax.dot_general(
        vectors,
        matrix,
        (((1,), (1,)), ((), ())),
        precision=lax.Precision.HIGHEST,
        preferred_element_type=jnp.float32,
    )


def body(
    leaf_rhs, sep_rhs, leaf_inverse, sep_inverse, leaf_block, sep_block, pattern, outer_solution
):
    group_count = lax.axis_size("leaf")
    depth = group_count.bit_length() - 1
    group_pos = lax.axis_index("leaf")
    front_pos = lax.axis_index("front")
    local_rows = leaf_rhs.shape[-1]
    full_rows = leaf_inverse.shape[-1]
    vector_count = leaf_rhs.shape[1]
    leaf_r = leaf_rhs[0]
    leaf_inv = leaf_inverse[0]
    leaf_u = leaf_block[0]
    sep_r = sep_rhs[0]
    sep_inv = sep_inverse[0]
    sep_u = sep_block[0]
    all_rows = jnp.arange(full_rows, dtype=jnp.int32)

    def geometry(level):
        blocks = 2 ** min(level, depth)
        share = local_rows // blocks
        offset = local_rows - (local_rows >> level - 1)
        return (share, offset, group_pos % blocks)

    def label_of(level):
        if level > depth:
            return jnp.int32(0)
        return group_pos // 2**level * 2**level + 2 ** (level - 1)

    def ids_of(level):
        return lax.dynamic_index_in_dim(pattern[1], label_of(level), 0, keepdims=False)

    def block_sum(term, level):
        nbits = min(level, depth)
        if nbits == depth:
            return lax.psum(term, ("leaf", "front"))
        piece = lax.psum_scatter(term, "front", scatter_dimension=1, tiled=True)
        for bit in range(nbits):
            piece = piece + partner(piece, "leaf", bit)
        return lax.all_gather(piece, "front", axis=1, tiled=True)

    leaf_y = against_rows(lax.all_gather(leaf_r, "front", axis=1, tiled=True), leaf_inv)
    leaf_ids = lax.dynamic_index_in_dim(pattern[0], group_pos, 0, keepdims=False)
    child_part = against_rows(leaf_y, leaf_u)
    child_ids = leaf_ids
    solved = {}
    for level in range(1, depth + 2):
        share, offset, inner_pos = geometry(level)
        own_r = sep_r[:, offset : offset + share]
        start_col = front_pos * local_rows + inner_pos * share
        contribution = jnp.zeros((vector_count, full_rows), jnp.float32)
        contribution = lax.dynamic_update_slice(contribution, own_r, (jnp.int32(0), start_col))
        selector = (child_ids[:, None] == all_rows[None, :]).astype(jnp.float32)
        contribution = contribution - times_rows(child_part, selector)
        whole_v = block_sum(contribution, level)
        y_level = against_rows(whole_v, sep_inv[offset : offset + share, :])
        solved[level] = y_level
        if level <= depth:
            child_part = against_rows(y_level, sep_u[:, offset : offset + share])
            child_ids = ids_of(level)
    parent_x = lax.all_gather(outer_solution, "front", axis=1, tiled=True)
    sep_full = jnp.zeros((vector_count, full_rows), jnp.float32)
    for level in range(depth + 1, 0, -1):
        share, offset, inner_pos = geometry(level)
        picked = jnp.take(parent_x, ids_of(level), axis=1)
        rest = solved[level] - times_rows(picked, sep_u[:, offset : offset + share])
        term = times_rows(rest, sep_inv[offset : offset + share, :])
        parent_x = block_sum(term, level)
        sep_full = jnp.where(label_of(level) == group_pos, parent_x, sep_full)
    picked = jnp.take(parent_x, leaf_ids, axis=1)
    rest = leaf_y - times_rows(picked, leaf_u)
    leaf_x = lax.psum_scatter(times_rows(rest, leaf_inv), "front", scatter_dimension=1, tiled=True)
    sep_x = lax.dynamic_slice_in_dim(sep_full, front_pos * local_rows, local_rows, 1)
    return jnp.stack([leaf_x, sep_x])[:, None]


def solution(mesh):
    placed = (
        P("leaf", None, "front"),
        P("leaf", None, "front"),
        P("leaf", "front", None),
        P("leaf", "front", None),
        P("leaf", None, "front"),
        P("leaf", None, "front"),
        P(),
        P(None, "front"),
    )
    return jax.shard_map(
        body, mesh=mesh, in_specs=placed, out_specs=P(None, "leaf", None, "front"), check_vma=False
    )
```

profile of v0, /device:TPU:0, one launch (start us, length us, event | category | flops | bytes accessed | tf_op | source)
XLA Modules:
  0.0 694.5 jit_solution(14276887811836147891)
XLA Ops:
  6.6 0.7 copy-done.9
  7.4 15.1 %all-gather = f32[1,64,256]{1,0,2:T(1,128)S(1)} all-gather(f32[1,64,64]{1,0,2:T(1,128)S(1)} %copy.15), channel_id=2, replica_groups=mesh['leaf'=8,'front'=4] {'front'}, dimensions={2}, use_global_device_ids=true | all-gather | bytes 81920 | tf_op jit(solution)/shard_map/all_gather | solution.py:74
  22.5 0.4 fusion.1
  22.9 0.3 copy-done.6
  23.4 0.7 copy-done.1
  24.1 0.4 dynamic_update_slice.12
  24.8 0.7 copy.26
  25.6 20.6 %reduce-scatter.16.cloned.1.call-done = f32[64,64]{1,0:T(8,128)} async-done(((f32[256,64]{1,0:T(8,128)}), f32[64,64]{1,0:T(8,128)}) %reduce-scatter.16.cloned.1.call-update) | async-done | bytes 16400
  46.2 0.8 copy.27
  47.2 0.4 dynamic_update_slice.13
  47.7 0.6 collective-permute-done
  48.4 13.5 %all_gather.19 = f32[64,256]{0,1:T(8,128)S(1)} all-gather(f32[64,64]{0,1:T(8,128)S(1)} %copy.16), channel_id=1, replica_groups=mesh['leaf'=8,'front'=4] {'front'}, dimensions={1}, use_global_device_ids=true | all-gather | bytes 81920 | tf_op jit(solution)/shard_map/all_gather | solution.py:72
  62.1 0.5 copy-done.2
  63.1 0.7 copy.28
  64.0 17.4 %reduce-scatter.18.cloned.1.call-done = f32[64,64]{1,0:T(8,128)} async-done(((f32[256,64]{1,0:T(8,128)}), f32[64,64]{1,0:T(8,128)}) %reduce-scatter.18.cloned.1.call-update) | async-done | bytes 16400
  81.4 0.8 copy.29
  82.3 1.2 collective-permute-done.1
  83.5 1.5 collective-permute-start.2
  85.0 0.4 dynamic_update_slice.14
  85.5 2.0 collective-permute-done.2
  87.5 13.4 %all_gather.20 = f32[64,256]{0,1:T(8,128)S(1)} all-gather(f32[64,64]{0,1:T(8,128)S(1)} %copy.17), channel_id=1, replica_groups=mesh['leaf'=8,'front'=4] {'front'}, dimensions={1}, use_global_device_ids=true | all-gather | bytes 81920 | tf_op jit(solution)/shard_map/all_gather | solution.py:72
  101.1 0.3 fusion.36
  101.4 0.9 convolution_subtract_fusion.1
  102.3 0.4 dynamic_update_slice.15
  102.8 115.3 %all-reduce.5.cloned.1.call-done = f32[64,256]{1,0:T(8,128)} async-done(((f32[64,256]{1,0:T(8,128)}), f32[64,256]{1,0:T(8,128)}) %all-reduce.5.cloned.1.call-update) | async-done | bytes 65552 | tf_op jit(solution)/shard_map/psum | solution.py:68
  218.1 1.0 fusion.49
  219.0 0.3 fusion.33
  219.3 0.9 convolution_subtract_fusion
  220.3 0.7 copy-done.8
  221.0 14.3 %all_gather.21 = f32[64,256]{0,1:T(8,128)S(1)} all-gather(f32[64,64]{0,1:T(8,128)S(1)} %copy.18), channel_id=1, replica_groups=mesh['leaf'=8,'front'=4] {'front'}, dimensions={1}, use_global_device_ids=true | all-gather | bytes 81920 | tf_op jit(solution)/shard_map/all_gather | solution.py:93
  235.4 0.6 gather_fusion
  235.9 105.9 %all-reduce.7.cloned.1.call-done = f32[64,256]{1,0:T(8,128)} async-done(((f32[64,256]{1,0:T(8,128)}), f32[64,256]{1,0:T(8,128)}) %all-reduce.7.cloned.1.call-update) | async-done | bytes 65552 | tf_op jit(solution)/shard_map/psum | solution.py:68
  341.9 1.0 fusion.45
  342.9 0.3 convolution_subtract_fusion.5
  343.2 0.8 fusion.43
  344.1 121.5 %all-reduce.9.cloned.1.call-done = f32[64,256]{1,0:T(8,128)} async-done(((f32[64,256]{1,0:T(8,128)}), f32[64,256]{1,0:T(8,128)}) %all-reduce.9.cloned.1.call-update) | async-done | bytes 65552 | tf_op jit(solution)/shard_map/psum | solution.py:68
  465.6 0.9 copy.19
  466.6 0.6 gather_fusion.1
  467.2 0.3 convolution_subtract_fusion.8
  467.4 0.9 fusion.47
  468.4 121.0 %all-reduce.11.cloned.1.call-done = f32[64,256]{1,0:T(8,128)} async-done(((f32[64,256]{1,0:T(8,128)}), f32[64,256]{1,0:T(8,128)}) %all-reduce.11.cloned.1.call-update) | async-done | bytes 65552 | tf_op jit(solution)/shard_map/psum | solution.py:68
  589.4 0.9 copy.20
  590.4 0.6 gather_fusion.2
  591.0 0.3 convolution_subtract_fusion.7
  591.2 1.1 convolution_bitcast_fusion.2
  592.4 20.0 %reduce-scatter.20.cloned.1.call-done = f32[64,64]{1,0:T(8,128)} async-done(((f32[256,64]{1,0:T(8,128)}), f32[64,64]{1,0:T(8,128)}) %reduce-scatter.20.cloned.1.call-update) | async-done | bytes 16400
  612.4 0.8 copy.31
  613.3 1.2 collective-permute-done.3
  614.5 1.6 collective-permute-start.4
  616.0 2.3 collective-permute-done.4
  618.5 13.3 %all_gather.22 = f32[64,256]{0,1:T(8,128)S(1)} all-gather(f32[64,64]{0,1:T(8,128)S(1)} %copy.21), channel_id=1, replica_groups=mesh['leaf'=8,'front'=4] {'front'}, dimensions={1}, use_global_device_ids=true | all-gather | bytes 81920 | tf_op jit(solution)/shard_map/all_gather | solution.py:72
  631.8 0.6 gather_fusion.3
  632.6 1.0 convolution_bitcast_fusion.1
  633.8 17.6 %reduce-scatter.22.cloned.1.call-done = f32[64,64]{1,0:T(8,128)} async-done(((f32[256,64]{1,0:T(8,128)}), f32[64,64]{1,0:T(8,128)}) %reduce-scatter.22.cloned.1.call-update) | async-done | bytes 16400
  651.3 0.8 copy.33
  652.3 1.1 collective-permute-done.5
  653.5 13.4 %all_gather.23 = f32[64,256]{0,1:T(8,128)S(1)} all-gather(f32[64,64]{0,1:T(8,128)S(1)} %copy.22), channel_id=1, replica_groups=mesh['leaf'=8,'front'=4] {'front'}, dimensions={1}, use_global_device_ids=true | all-gather | bytes 81920 | tf_op jit(solution)/shard_map/all_gather | solution.py:72
  666.9 0.6 gather_fusion.4
  667.5 0.3 convolution_subtract_fusion.4
  667.9 1.0 convolution_bitcast_fusion
  668.9 0.8 copy-done.4
  669.9 16.6 %reduce-scatter.24.cloned.1.call-done = f32[64,64]{1,0:T(8,128)} async-done(((f32[256,64]{1,0:T(8,128)}), f32[64,64]{1,0:T(8,128)}) %reduce-scatter.24.cloned.1.call-update) | async-done | bytes 16400
  686.5 0.8 copy.35
  687.3 0.6 maximum_bitcast_fusion
  (79 shorter events, 3.3 us)
Async XLA Ops:
  6.5 15.9 %copy-start = (f32[1,64,256]{2,1,0:T(8,128)S(1)}, f32[1,64,256]{2,1,0:T(8,128)}, u32[]{:S(2)}) copy-start(f32[1,64,256]{2,1,0:T(8,128)} %param.12) | copy-start | bytes 196612
  6.5 0.8 copy-start.7
  6.5 39.7 %reduce-scatter.16.cloned.1.call-start = ((), (), s32[]{:S(2)}) async-start(), calls=%async_computation.9 | async-start | bytes 163840
  6.5 0.7 copy-start.9
  22.5 0.7 copy-start.6
  23.4 0.8 copy-start.1
  25.5 55.9 %reduce-scatter.18.cloned.1.call-start = ((), (), s32[]{:S(2)}) async-start(), calls=%async_computation.10 | async-start | bytes 163840
  47.0 1.3 collective-permute-start
  48.4 13.5 %copy-start.3 = (f32[1,64,256]{2,1,0:T(8,128)S(1)}, f32[1,64,256]{2,1,0:T(8,128)}, u32[]{:S(2)}) copy-start(f32[1,64,256]{2,1,0:T(8,128)} %param.13) | copy-start | bytes 196612
  61.9 0.7 copy-start.2
  63.9 154.2 %all-reduce.5.cloned.1.call-start = ((), (), s32[]{:S(2)}) async-start(), calls=%async_computation.5 | async-start | bytes 131072 | tf_op jit(solution)/shard_map/psum | solution.py:68
  82.2 1.3 collective-permute-start.1
  83.5 3.9 collective-permute-start.2
  102.3 239.6 %all-reduce.7.cloned.1.call-start = ((), (), s32[]{:S(2)}) async-start(), calls=%async_computation.6 | async-start | bytes 131072 | tf_op jit(solution)/shard_map/psum | solution.py:68
  220.2 0.8 copy-start.8
  220.2 245.4 %all-reduce.9.cloned.1.call-start = ((), (), s32[]{:S(2)}) async-start(), calls=%async_computation.7 | async-start | bytes 131072 | tf_op jit(solution)/shard_map/psum | solution.py:68
  344.0 245.4 %all-reduce.11.cloned.1.call-start = ((), (), s32[]{:S(2)}) async-start(), calls=%async_computation.8 | async-start | bytes 131072 | tf_op jit(solution)/shard_map/psum | solution.py:68
  468.4 144.0 %reduce-scatter.20.cloned.1.call-start = ((), (), s32[]{:S(2)}) async-start(), calls=%async_computation.11 | async-start | bytes 163840
  592.3 59.0 %reduce-scatter.22.cloned.1.call-start = ((), (), s32[]{:S(2)}) async-start(), calls=%async_computation.12 | async-start | bytes 163840
  613.2 1.3 collective-permute-start.3
  614.5 3.9 collective-permute-start.4
  633.7 52.8 %reduce-scatter.24.cloned.1.call-start = ((), (), s32[]{:S(2)}) async-start(), calls=%async_computation.13 | async-start | bytes 163840
  652.2 1.3 collective-permute-start.5
  668.9 0.8 copy-start.4
  668.9 0.9 copy-start.5
Sparse Core Ops, SparseCore 0:
  25.6 20.5 reduce-scatter.15
  64.0 17.3 reduce-scatter.17
  102.4 115.6 all-reduce.4
  223.5 118.3 all-reduce.6
  347.3 118.3 all-reduce.8
  471.1 118.3 all-reduce.10
  592.4 19.9 reduce-scatter.19
  633.8 17.4 reduce-scatter.21
  669.1 17.4 reduce-scatter.23
where the time goes:
time: 696 us; the launch traced here: 695 us
  waiting for transfers between devices  565 us (81%)
  blocking collectives  83.1 us (12%)
  local copies, waits for them, and re-layouts  16.8 us (2%)
  between operations  13.6 us (2%)
  matrix products  12.1 us (2%)
    psum x4, waiting for transfers between devices, block_sum(): return lax.psum(term, ('leaf', 'front'))  464 us
    unnamed x14, waiting for transfers between devices  92.4 us
    all_gather x4, blocking collectives, block_sum(): return lax.all_gather(piece, 'front', axis=1, tiled=True)  53.7 us
    all_gather x1, blocking collectives, body(): lax.all_gather(leaf_r, 'front', axis=1, tiled=True)  15.1 us
    all_gather x1, blocking collectives, body(): parent_x = lax.all_gather(outer_solution, 'front', axis=1, tiled=True)  14.3 us
  transfers between devices with their start and end apart: 15, of which 15 were waited for; matrix products, arithmetic and copies ran while one was open for 0% of the time, Pallas kernels for 0%

commit v1 on v0

--- a/solution.py
+++ b/solution.py
@@ -65,7 +65,7 @@
     def block_sum(term, level):
         nbits = min(level, depth)
         if nbits == depth:
-            return lax.psum(term, ("leaf", "front"))
+            return lax.psum(lax.psum(term, "front"), "leaf")
         piece = lax.psum_scatter(term, "front", scatter_dimension=1, tiled=True)
         for bit in range(nbits):
             piece = piece + partner(piece, "leaf", bit)

time: 696 us -> 569 us (0.82)
  waiting for transfers between devices: 565 us -> 438 us
    psum x4 -> x8, waiting for transfers between devices: 464 us -> 339 us  [block_sum(): return lax.psum(lax.psum(term, 'front'), 'leaf')]
    unnamed x14 -> x18, waiting for transfers between devices: 92.4 us -> 91.1 us
  transfers between devices with their start and end apart: 15 -> 19, of which waited for: 15 -> 19; matrix products, arithmetic and copies ran while one was open for 0% -> 0% of each run, Pallas kernels for 0% -> 0%
where the time goes in v1:
time: 569 us; the launch traced here: 568 us
  waiting for transfers between devices  438 us (77%)
  blocking collectives  82.4 us (14%)
  local copies, waits for them, and re-layouts  16.8 us (3%)
  between operations  13.7 us (2%)
  matrix products  12.1 us (2%)
    psum x8, waiting for transfers between devices, block_sum(): return lax.psum(lax.psum(term, 'front'), 'leaf')  339 us
    unnamed x18, waiting for transfers between devices  91.1 us
    all_gather x4, blocking collectives, block_sum(): return lax.all_gather(piece, 'front', axis=1, tiled=True)  53.7 us
    all_gather x1, blocking collectives, body(): lax.all_gather(leaf_r, 'front', axis=1, tiled=True)  15.1 us
    all_gather x1, blocking collectives, body(): parent_x = lax.all_gather(outer_solution, 'front', axis=1, tiled=True)  13.6 us
  transfers between devices with their start and end apart: 19, of which 19 were waited for; matrix products, arithmetic and copies ran while one was open for 0% of the time, Pallas kernels for 0%

profile of v1, /device:TPU:0, one launch (start us, length us, event | category | flops | bytes accessed | tf_op | source)
XLA Modules:
  0.0 567.6 jit_solution(4279874988563743234)
XLA Ops:
  6.6 0.7 copy-done.9
  7.4 15.1 %all-gather = f32[1,64,256]{1,0,2:T(1,128)S(1)} all-gather(f32[1,64,64]{1,0,2:T(1,128)S(1)} %copy.15), channel_id=2, replica_groups=mesh['leaf'=8,'front'=4] {'front'}, dimensions={2}, use_global_device_ids=true | all-gather | bytes 81920 | tf_op jit(solution)/shard_map/all_gather | solution.py:74
  22.5 0.4 fusion.1
  22.9 0.3 copy-done.6
  23.4 0.7 copy-done.1
  24.1 0.4 dynamic_update_slice.12
  24.8 0.7 copy.26
  25.6 20.6 %reduce-scatter.16.cloned.1.call-done = f32[64,64]{1,0:T(8,128)} async-done(((f32[256,64]{1,0:T(8,128)}), f32[64,64]{1,0:T(8,128)}) %reduce-scatter.16.cloned.1.call-update) | async-done | bytes 16400
  46.2 0.8 copy.27
  47.2 0.4 dynamic_update_slice.13
  47.7 0.6 collective-permute-done
  48.4 13.5 %all_gather.19 = f32[64,256]{0,1:T(8,128)S(1)} all-gather(f32[64,64]{0,1:T(8,128)S(1)} %copy.16), channel_id=1, replica_groups=mesh['leaf'=8,'front'=4] {'front'}, dimensions={1}, use_global_device_ids=true | all-gather | bytes 81920 | tf_op jit(solution)/shard_map/all_gather | solution.py:72
  62.1 0.5 copy-done.2
  63.1 0.7 copy.28
  63.9 17.5 %reduce-scatter.18.cloned.1.call-done = f32[64,64]{1,0:T(8,128)} async-done(((f32[256,64]{1,0:T(8,128)}), f32[64,64]{1,0:T(8,128)}) %reduce-scatter.18.cloned.1.call-update) | async-done | bytes 16400
  81.4 0.8 copy.29
  82.3 1.2 collective-permute-done.1
  83.5 1.5 collective-permute-start.2
  85.1 0.4 dynamic_update_slice.14
  85.5 1.9 collective-permute-done.2
  87.5 13.4 %all_gather.20 = f32[64,256]{0,1:T(8,128)S(1)} all-gather(f32[64,64]{0,1:T(8,128)S(1)} %copy.17), channel_id=1, replica_groups=mesh['leaf'=8,'front'=4] {'front'}, dimensions={1}, use_global_device_ids=true | all-gather | bytes 81920 | tf_op jit(solution)/shard_map/all_gather | solution.py:72
  101.4 0.9 convolution_subtract_fusion.1
  102.3 32.3 %all-reduce.9.cloned.1.call-done = f32[64,256]{1,0:T(8,128)} async-done(((f32[64,256]{1,0:T(8,128)}), f32[64,256]{1,0:T(8,128)}) %all-reduce.9.cloned.1.call-update) | async-done | bytes 65552 | tf_op jit(solution)/shard_map/psum | solution.py:68
  134.7 0.4 dynamic_update_slice.15
  135.1 54.8 %all-reduce.11.cloned.1.call-done = f32[64,256]{1,0:T(8,128)} async-done(((f32[64,256]{1,0:T(8,128)}), f32[64,256]{1,0:T(8,128)}) %all-reduce.11.cloned.1.call-update) | async-done | bytes 65552 | tf_op jit(solution)/shard_map/psum | solution.py:68
  190.0 1.0 fusion.49
  191.2 0.9 convolution_subtract_fusion
  192.2 33.5 %all-reduce.13.cloned.1.call-done = f32[64,256]{1,0:T(8,128)} async-done(((f32[64,256]{1,0:T(8,128)}), f32[64,256]{1,0:T(8,128)}) %all-reduce.13.cloned.1.call-update) | async-done | bytes 65552 | tf_op jit(solution)/shard_map/psum | solution.py:68
  225.7 0.7 copy-done.8
  226.5 13.6 %all_gather.21 = f32[64,256]{0,1:T(8,128)S(1)} all-gather(f32[64,64]{0,1:T(8,128)S(1)} %copy.18), channel_id=1, replica_groups=mesh['leaf'=8,'front'=4] {'front'}, dimensions={1}, use_global_device_ids=true | all-gather | bytes 81920 | tf_op jit(solution)/shard_map/all_gather | solution.py:93
  240.1 0.6 gather_fusion
  240.7 40.4 %all-reduce.15.cloned.1.call-done = f32[64,256]{1,0:T(8,128)} async-done(((f32[64,256]{1,0:T(8,128)}), f32[64,256]{1,0:T(8,128)}) %all-reduce.15.cloned.1.call-update) | async-done | bytes 65552 | tf_op jit(solution)/shard_map/psum | solution.py:68
  281.0 1.0 fusion.45
  282.0 0.3 convolution_subtract_fusion.5
  282.4 0.8 fusion.43
  283.3 33.5 %all-reduce.17.cloned.1.call-done = f32[64,256]{1,0:T(8,128)} async-done(((f32[64,256]{1,0:T(8,128)}), f32[64,256]{1,0:T(8,128)}) %all-reduce.17.cloned.1.call-update) | async-done | bytes 65552 | tf_op jit(solution)/shard_map/psum | solution.py:68
  316.8 55.4 %all-reduce.19.cloned.1.call-done = f32[64,256]{1,0:T(8,128)} async-done(((f32[64,256]{1,0:T(8,128)}), f32[64,256]{1,0:T(8,128)}) %all-reduce.19.cloned.1.call-update) | async-done | bytes 65552 | tf_op jit(solution)/shard_map/psum | solution.py:68
  372.2 0.9 copy.19
  373.2 0.6 gather_fusion.1
  374.0 0.9 fusion.47
  375.0 33.5 %all-reduce.21.cloned.1.call-done = f32[64,256]{1,0:T(8,128)} async-done(((f32[64,256]{1,0:T(8,128)}), f32[64,256]{1,0:T(8,128)}) %all-reduce.21.cloned.1.call-update) | async-done | bytes 65552 | tf_op jit(solution)/shard_map/psum | solution.py:68
  408.6 55.3 %all-reduce.23.cloned.1.call-done = f32[64,256]{1,0:T(8,128)} async-done(((f32[64,256]{1,0:T(8,128)}), f32[64,256]{1,0:T(8,128)}) %all-reduce.23.cloned.1.call-update) | async-done | bytes 65552 | tf_op jit(solution)/shard_map/psum | solution.py:68
  463.8 0.9 copy.20
  464.8 0.6 gather_fusion.2
  465.6 1.1 convolution_bitcast_fusion.2
  466.7 18.7 %reduce-scatter.20.cloned.1.call-done = f32[64,64]{1,0:T(8,128)} async-done(((f32[256,64]{1,0:T(8,128)}), f32[64,64]{1,0:T(8,128)}) %reduce-scatter.20.cloned.1.call-update) | async-done | bytes 16400
  485.4 0.8 copy.31
  486.3 1.2 collective-permute-done.3
  487.5 1.5 collective-permute-start.4
  489.0 2.4 collective-permute-done.4
  491.5 13.3 %all_gather.22 = f32[64,256]{0,1:T(8,128)S(1)} all-gather(f32[64,64]{0,1:T(8,128)S(1)} %copy.21), channel_id=1, replica_groups=mesh['leaf'=8,'front'=4] {'front'}, dimensions={1}, use_global_device_ids=true | all-gather | bytes 81920 | tf_op jit(solution)/shard_map/all_gather | solution.py:72
  504.9 0.6 gather_fusion.3
  505.7 1.0 convolution_bitcast_fusion.1
  506.8 17.6 %reduce-scatter.22.cloned.1.call-done = f32[64,64]{1,0:T(8,128)} async-done(((f32[256,64]{1,0:T(8,128)}), f32[64,64]{1,0:T(8,128)}) %reduce-scatter.22.cloned.1.call-update) | async-done | bytes 16400
  524.4 0.8 copy.33
  525.4 1.1 collective-permute-done.5
  526.6 13.4 %all_gather.23 = f32[64,256]{0,1:T(8,128)S(1)} all-gather(f32[64,64]{0,1:T(8,128)S(1)} %copy.22), channel_id=1, replica_groups=mesh['leaf'=8,'front'=4] {'front'}, dimensions={1}, use_global_device_ids=true | all-gather | bytes 81920 | tf_op jit(solution)/shard_map/all_gather | solution.py:72
  540.0 0.6 gather_fusion.4
  540.6 0.3 convolution_subtract_fusion.4
  540.9 1.0 convolution_bitcast_fusion
  542.0 0.8 copy-done.4
  542.9 16.6 %reduce-scatter.24.cloned.1.call-done = f32[64,64]{1,0:T(8,128)} async-done(((f32[256,64]{1,0:T(8,128)}), f32[64,64]{1,0:T(8,128)}) %reduce-scatter.24.cloned.1.call-update) | async-done | bytes 16400
  559.6 0.8 copy.35
  560.4 0.6 maximum_bitcast_fusion
  (91 shorter events, 4.6 us)
Async XLA Ops:
  6.5 15.9 %copy-start = (f32[1,64,256]{2,1,0:T(8,128)S(1)}, f32[1,64,256]{2,1,0:T(8,128)}, u32[]{:S(2)}) copy-start(f32[1,64,256]{2,1,0:T(8,128)} %param.12) | copy-start | bytes 196612
  6.5 0.8 copy-start.7
  6.5 39.7 %reduce-scatter.16.cloned.1.call-start = ((), (), s32[]{:S(2)}) async-start(), calls=%async_computation.13 | async-start | bytes 163840
  6.5 0.7 copy-start.9
  22.5 0.7 copy-start.6
  23.4 0.8 copy-start.1
  25.5 55.9 %reduce-scatter.18.cloned.1.call-start = ((), (), s32[]{:S(2)}) async-start(), calls=%async_computation.14 | async-start | bytes 163840
  47.0 1.3 collective-permute-start
  48.4 13.5 %copy-start.3 = (f32[1,64,256]{2,1,0:T(8,128)S(1)}, f32[1,64,256]{2,1,0:T(8,128)}, u32[]{:S(2)}) copy-start(f32[1,64,256]{2,1,0:T(8,128)} %param.13) | copy-start | bytes 196612
  61.9 0.7 copy-start.2
  63.9 70.7 %all-reduce.9.cloned.1.call-start = ((), (), s32[]{:S(2)}) async-start(), calls=%async_computation.5 | async-start | bytes 131072 | tf_op jit(solution)/shard_map/psum | solution.py:68
  82.2 1.3 collective-permute-start.1
  83.5 3.9 collective-permute-start.2
  102.3 87.7 %all-reduce.11.cloned.1.call-start = ((), (), s32[]{:S(2)}) async-start(), calls=%async_computation.6 | async-start | bytes 131072 | tf_op jit(solution)/shard_map/psum | solution.py:68
  134.6 91.0 %all-reduce.13.cloned.1.call-start = ((), (), s32[]{:S(2)}) async-start(), calls=%async_computation.7 | async-start | bytes 131072 | tf_op jit(solution)/shard_map/psum | solution.py:68
  192.1 88.9 %all-reduce.15.cloned.1.call-start = ((), (), s32[]{:S(2)}) async-start(), calls=%async_computation.8 | async-start | bytes 131072 | tf_op jit(solution)/shard_map/psum | solution.py:68
  225.6 0.8 copy-start.8
  225.7 91.1 %all-reduce.17.cloned.1.call-start = ((), (), s32[]{:S(2)}) async-start(), calls=%async_computation.9 | async-start | bytes 131072 | tf_op jit(solution)/shard_map/psum | solution.py:68
  283.2 89.0 %all-reduce.19.cloned.1.call-start = ((), (), s32[]{:S(2)}) async-start(), calls=%async_computation.10 | async-start | bytes 131072 | tf_op jit(solution)/shard_map/psum | solution.py:68
  316.7 91.7 %all-reduce.21.cloned.1.call-start = ((), (), s32[]{:S(2)}) async-start(), calls=%async_computation.11 | async-start | bytes 131072 | tf_op jit(solution)/shard_map/psum | solution.py:68
  374.9 88.9 %all-reduce.23.cloned.1.call-start = ((), (), s32[]{:S(2)}) async-start(), calls=%async_computation.12 | async-start | bytes 131072 | tf_op jit(solution)/shard_map/psum | solution.py:68
  408.5 76.9 %reduce-scatter.20.cloned.1.call-start = ((), (), s32[]{:S(2)}) async-start(), calls=%async_computation.15 | async-start | bytes 163840
  466.7 57.7 %reduce-scatter.22.cloned.1.call-start = ((), (), s32[]{:S(2)}) async-start(), calls=%async_computation.16 | async-start | bytes 163840
  486.3 1.3 collective-permute-start.3
  487.5 3.9 collective-permute-start.4
  506.7 52.8 %reduce-scatter.24.cloned.1.call-start = ((), (), s32[]{:S(2)}) async-start(), calls=%async_computation.17 | async-start | bytes 163840
  525.2 1.3 collective-permute-start.5
  542.0 0.8 copy-start.4
  542.0 0.9 copy-start.5
Sparse Core Ops, SparseCore 0:
  25.6 20.5 reduce-scatter.15
  64.0 17.3 reduce-scatter.17
  102.4 32.1 all-reduce.8
  137.8 52.1 all-reduce.10
  192.2 33.3 all-reduce.12
  228.8 52.1 all-reduce.14
  283.3 33.3 all-reduce.16
  320.1 52.1 all-reduce.18
  375.1 33.3 all-reduce.20
  411.7 52.1 all-reduce.22
  466.8 18.5 reduce-scatter.19
  506.9 17.4 reduce-scatter.21
  542.1 17.3 reduce-scatter.23
